TPU v7x, 256 devices: a whole 4x4x8 slice. The times are simulated.
256 devices in a mesh: leaf: 32 (over x, z), sub: 8 (over y, core).
Axes of the slice: x: 4, y: 4, z: 8, core: 2. Of those that a mesh axis runs over, the one named last changes fastest.
Arguments:
- leaf_right: bfloat16 [1024, 512, 256], P(('leaf', 'sub')), may hold values from -6 to 6
- leaf_inverse: bfloat16 [1024, 512, 512], P(('leaf', 'sub')), may hold values from -2.5 to 2.5, as said below
- panels: bfloat16 [1024, 256, 512], P(('leaf', 'sub')), may hold values from -0.125 to 0.125
- leaf_subtree: int32 [1024], P(('leaf', 'sub')), may hold values from 0 to 31, as said below
- panel_block: int32 [1024, 4], P(('leaf', 'sub')), may hold values from 0 to 63
- separator_right: bfloat16 [131072, 256], P(('leaf', 'sub')), may hold values from -6 to 6
- separator_inverse: bfloat16 [131072, 512], P(('leaf', 'sub')), may hold values from -2.5 to 2.5, as said below
- separator_factor: bfloat16 [131072, 4096], P(('leaf', 'sub')), may hold values from -1 to 1, as said below
Outputs:
- leaf_solution: bfloat16 [1024, 512, 256], P(('leaf', 'sub'))
- separator_solution: bfloat16 [131072, 256], P(('leaf', 'sub'))
Inputs may be any that keep to these rules, and one draw needn't show every extreme that they name: `leaf_subtree`: every leaf supernode held by section s of the leaf axis belongs to a subtree between s - (2) and s. Each device of section s holds, for every d from 0 to min(2, s), at least one leaf supernode of subtree s - d. `leaf_inverse`: each 512 x 512 block is lower triangular, with its diagonal between 0.6 and 1.4. `separator_inverse`: each 512 x 512 block is lower triangular, with its diagonal between 0.6 and 1.4. `separator_factor`: within each subtree's 4096 rows, the block of row block q and column block p (blocks of 512) is zero unless q > p.
All inputs are finite; a program needn't handle non-finite values.
Results may differ from a plain program's by a relative error of at most 0.024.
Values may be sent and summed in bfloat16 or wider, within the bound.
No kernel may reach another device: no remote copies, remote signals or barrier semaphores. Data moves between devices by JAX's collectives and lax.ppermute only.
A program may use at most 128 MiB of HBM per device.

v0:
```python
import jax
import jax.numpy as jnp
from jax import lax
from jax.sharding import PartitionSpec as P

WSN = 512
SA = 4096
R = 256
BLK = 64
KB = 4
SPAN = 3
exact_precision = lax.Precision.HIGHEST


def passed_along(block, axis, distance):
    devices = range(lax.axis_size(axis))
    route = [(i - distance, i) for i in devices if i - distance in devices]
    return lax.ppermute(block, axis, route)


def broadcast(shard, axis, root):
    mine = lax.axis_index(axis) == root
    return lax.psum(jnp.where(mine, shard, jnp.zeros_like(shard)), axis)


def route_forward(stacked):
    summed = stacked[0]
    for distance in range(1, SPAN):
        summed = summed + passed_along(stacked[distance], "leaf", -distance)
    return summed


def route_back(item):
    collected = [item] + [passed_along(item, "leaf", distance) for distance in range(1, SPAN)]
    return jnp.stack(collected)


def shards(
    leaf_right,
    leaf_inverse,
    panels,
    leaf_subtree,
    panel_block,
    separator_right,
    separator_inverse,
    separator_factor,
):
    section = lax.axis_index("leaf")
    member = lax.axis_index("sub")
    leaves_here = leaf_right.shape[0]
    row_blocks = SA // BLK
    share_rows = separator_right.shape[0]
    per_device = share_rows // WSN
    solved = jnp.einsum(
        "jab,jbr->jar", leaf_inverse, leaf_right, preferred_element_type=jnp.float32
    ).astype(jnp.bfloat16)
    updates = jnp.einsum(
        "jib,jbr->jir", panels, solved, preferred_element_type=jnp.float32
    ).reshape(leaves_here * KB, BLK * R)
    offsets = section - leaf_subtree
    slot_index = (offsets[:, None] * row_blocks + panel_block).reshape(-1)
    selector = (
        jnp.arange(SPAN * row_blocks, dtype=jnp.int32)[:, None] == slot_index[None, :]
    ).astype(jnp.float32)
    spilled = jnp.dot(
        selector, updates, precision=exact_precision, preferred_element_type=jnp.float32
    ).reshape(SPAN, SA, R)
    own_rows = lax.psum_scatter(route_forward(spilled), "sub", scatter_dimension=0, tiled=True)
    rhs_rows = (separator_right.astype(jnp.float32) - own_rows).astype(jnp.bfloat16)
    inverse_blocks = separator_inverse.reshape(per_device, WSN, WSN)
    running = rhs_rows.astype(jnp.float32).reshape(per_device, WSN, R)
    empty_block = jnp.zeros((WSN, R), jnp.bfloat16)
    forward_store = jnp.zeros((per_device, WSN, R), jnp.bfloat16)
    for column in range(SA // WSN):
        owner = column // per_device
        local_col = column % per_device
        is_owner = member == owner

        def solve_block():
            return jnp.dot(
                inverse_blocks[local_col].astype(jnp.float32),
                running[local_col],
                precision=exact_precision,
                preferred_element_type=jnp.float32,
            ).astype(jnp.bfloat16)

        own_block = lax.cond(is_owner, solve_block, lambda: empty_block)
        block_y = broadcast(own_block, "sub", owner)
        forward_store = forward_store.at[local_col].set(
            jnp.where(is_owner, block_y, forward_store[local_col])
        )
        column_panel = separator_factor[:, column * WSN : (column + 1) * WSN]
        running = running - jnp.dot(
            column_panel, block_y, preferred_element_type=jnp.float32
        ).reshape(per_device, WSN, R)
    backward_store = jnp.zeros((per_device, WSN, R), jnp.bfloat16)
    for column in reversed(range(SA // WSN)):
        owner = column // per_device
        local_col = column % per_device
        is_owner = member == owner
        column_panel = separator_factor[:, column * WSN : (column + 1) * WSN]
        partial_term = lax.dot_general(
            column_panel,
            backward_store.reshape(share_rows, R),
            (((0,), (0,)), ((), ())),
            preferred_element_type=jnp.float32,
        )
        summed_later = lax.psum(partial_term, "sub")

        def back_block():
            bracket = forward_store[local_col].astype(jnp.float32) - summed_later
            return lax.dot_general(
                inverse_blocks[local_col].astype(jnp.float32),
                bracket,
                (((0,), (0,)), ((), ())),
                precision=exact_precision,
                preferred_element_type=jnp.float32,
            ).astype(jnp.bfloat16)

        own_back = lax.cond(is_owner, back_block, lambda: empty_block)
        backward_store = backward_store.at[local_col].set(
            jnp.where(is_owner, own_back, backward_store[local_col])
        )
    separator_x = backward_store.reshape(share_rows, R)
    solution_table = route_back(lax.all_gather(separator_x, "sub", axis=0, tiled=True))
    pieces = jnp.take(solution_table.reshape(SPAN * row_blocks, BLK * R), slot_index, axis=0)
    pieces = pieces.reshape(leaves_here, KB * BLK, R)
    reduced = jnp.einsum("jib,jir->jbr", panels, pieces, preferred_element_type=jnp.float32)
    inner_rhs = (solved.astype(jnp.float32) - reduced).astype(jnp.bfloat16)
    leaf_x = jnp.einsum(
        "jab,jar->jbr", leaf_inverse, inner_rhs, preferred_element_type=jnp.float32
    ).astype(jnp.bfloat16)
    return (leaf_x, separator_x)


def solution(mesh):
    placed = (
        P(("leaf", "sub"), None, None),
        P(("leaf", "sub"), None, None),
        P(("leaf", "sub"), None, None),
        P(("leaf", "sub")),
        P(("leaf", "sub"), None),
        P(("leaf", "sub"), None),
        P(("leaf", "sub"), None),
        P(("leaf", "sub"), None),
    )
    return jax.shard_map(
        shards,
        mesh=mesh,
        in_specs=placed,
        out_specs=(P(("leaf", "sub"), None, None), P(("leaf", "sub"), None)),
        check_vma=False,
    )
```

profile of v0, /device:TPU:34, one launch (start us, length us, event | category | flops | bytes accessed | tf_op | source)
XLA Modules:
  0.0 1701.3 jit_solution(7460126840667194432)
XLA Ops:
  8.9 2.0 convolution_convert_fusion.17
  13.4 2.6 copy.45
  16.0 2.4 reshape.570
  18.4 9.1 fusion.50
  27.5 9.4 fusion.57
  36.9 4.9 squeeze.31
  41.8 5.7 copy.46
  47.4 2.0 collective-permute-start
  49.4 5.0 squeeze.32
  54.4 5.6 copy.48
  60.1 8.2 collective-permute-start.1
  68.2 5.0 squeeze.29
  73.2 5.6 copy.47
  78.8 64.7 %collective-permute-done = f32[4096,256]{0,1:T(8,128)} collective-permute-done((f32[4096,256]{0,1:T(8,128)}, f32[4096,256]{0,1:T(8,128)}, u32[]{:S(2)}, u32[]{:S(2)}) %collective-permute-start) | collective-permute-done | bytes 4194336 | tf_op jit(solution)/shard_map/ppermute | solution.py:18
  143.6 91.9 %collective-permute-done.1 = f32[4096,256]{0,1:T(8,128)} collective-permute-done((f32[4096,256]{0,1:T(8,128)}, f32[4096,256]{0,1:T(8,128)}, u32[]{:S(2)}, u32[]{:S(2)}) %collective-permute-start.1) | collective-permute-done | bytes 4194336 | tf_op jit(solution)/shard_map/ppermute | solution.py:18
  235.5 7.8 add_add_fusion
  244.4 130.0 %reduce-scatter.2.cloned.1.call-done = f32[512,256]{0,1:T(8,128)} async-done(((f32[4096,256]{0,1:T(8,128)}), f32[512,256]{0,1:T(8,128)}) %reduce-scatter.2.cloned.1.call-update) | async-done | bytes 524304 | tf_op jit(solution)/shard_map/reduce_scatter | solution.py:68
  374.4 1.9 fusion.45
  376.4 1.7 conditional.16
  376.4 1.7 convolution_convert_fusion
  378.9 63.9 %all-reduce.17.cloned.1.call-done = bf16[512,256]{1,0:T(8,128)(2,1)} async-done(((bf16[512,256]{1,0:T(8,128)(2,1)}), bf16[512,256]{1,0:T(8,128)(2,1)}) %all-reduce.17.cloned.1.call-update) | async-done | bytes 262160 | tf_op jit(solution)/shard_map/psum | solution.py:23
  442.8 1.6 fusion.20
  445.3 64.7 %all-reduce.19.cloned.1.call-done = bf16[512,256]{1,0:T(8,128)(2,1)} async-done(((bf16[512,256]{1,0:T(8,128)(2,1)}), bf16[512,256]{1,0:T(8,128)(2,1)}) %all-reduce.19.cloned.1.call-update) | async-done | bytes 262160 | tf_op jit(solution)/shard_map/psum | solution.py:23
  510.0 2.3 fusion.21
  513.1 64.3 %all-reduce.21.cloned.1.call-done = bf16[512,256]{1,0:T(8,128)(2,1)} async-done(((bf16[512,256]{1,0:T(8,128)(2,1)}), bf16[512,256]{1,0:T(8,128)(2,1)}) %all-reduce.21.cloned.1.call-update) | async-done | bytes 262160 | tf_op jit(solution)/shard_map/psum | solution.py:23
  577.4 1.6 fusion.22
  580.1 64.4 %all-reduce.23.cloned.1.call-done = bf16[512,256]{1,0:T(8,128)(2,1)} async-done(((bf16[512,256]{1,0:T(8,128)(2,1)}), bf16[512,256]{1,0:T(8,128)(2,1)}) %all-reduce.23.cloned.1.call-update) | async-done | bytes 262160 | tf_op jit(solution)/shard_map/psum | solution.py:23
  644.5 2.3 fusion.23
  647.6 64.2 %all-reduce.25.cloned.1.call-done = bf16[512,256]{1,0:T(8,128)(2,1)} async-done(((bf16[512,256]{1,0:T(8,128)(2,1)}), bf16[512,256]{1,0:T(8,128)(2,1)}) %all-reduce.25.cloned.1.call-update) | async-done | bytes 262160 | tf_op jit(solution)/shard_map/psum | solution.py:23
  711.8 1.6 fusion.24
  714.3 64.7 %all-reduce.27.cloned.1.call-done = bf16[512,256]{1,0:T(8,128)(2,1)} async-done(((bf16[512,256]{1,0:T(8,128)(2,1)}), bf16[512,256]{1,0:T(8,128)(2,1)}) %all-reduce.27.cloned.1.call-update) | async-done | bytes 262160 | tf_op jit(solution)/shard_map/psum | solution.py:23
  779.0 2.3 fusion.25
  782.1 65.5 %all-reduce.29.cloned.1.call-done = bf16[512,256]{1,0:T(8,128)(2,1)} async-done(((bf16[512,256]{1,0:T(8,128)(2,1)}), bf16[512,256]{1,0:T(8,128)(2,1)}) %all-reduce.29.cloned.1.call-update) | async-done | bytes 262160 | tf_op jit(solution)/shard_map/psum | solution.py:23
  847.6 2.3 convolution_bitcast_fusion.9
  851.4 2.2 convolution_bitcast_fusion.8
  853.7 70.1 %all-reduce.31.cloned.1.call-done = bf16[512,256]{1,0:T(8,128)(2,1)} async-done(((bf16[512,256]{1,0:T(8,128)(2,1)}), bf16[512,256]{1,0:T(8,128)(2,1)}) %all-reduce.31.cloned.1.call-update) | async-done | bytes 262160 | tf_op jit(solution)/shard_map/psum | solution.py:23
  923.9 67.1 %all-reduce.33.cloned.1.call-done = f32[512,256]{0,1:T(8,128)} async-done(((f32[512,256]{0,1:T(8,128)}), f32[512,256]{0,1:T(8,128)}) %all-reduce.33.cloned.1.call-update) | async-done | bytes 524304 | tf_op jit(solution)/shard_map/psum | solution.py:108
  991.7 2.2 convolution_bitcast_fusion.7
  994.0 69.0 %all-reduce.35.cloned.1.call-done = f32[512,256]{0,1:T(8,128)} async-done(((f32[512,256]{0,1:T(8,128)}), f32[512,256]{0,1:T(8,128)}) %all-reduce.35.cloned.1.call-update) | async-done | bytes 524304 | tf_op jit(solution)/shard_map/psum | solution.py:108
  1063.8 2.2 convolution_bitcast_fusion.6
  1066.0 69.4 %all-reduce.37.cloned.1.call-done = f32[512,256]{0,1:T(8,128)} async-done(((f32[512,256]{0,1:T(8,128)}), f32[512,256]{0,1:T(8,128)}) %all-reduce.37.cloned.1.call-update) | async-done | bytes 524304 | tf_op jit(solution)/shard_map/psum | solution.py:108
  1135.4 2.3 convolution_bitcast_fusion.5
  1137.8 68.9 %all-reduce.39.cloned.1.call-done = f32[512,256]{0,1:T(8,128)} async-done(((f32[512,256]{0,1:T(8,128)}), f32[512,256]{0,1:T(8,128)}) %all-reduce.39.cloned.1.call-update) | async-done | bytes 524304 | tf_op jit(solution)/shard_map/psum | solution.py:108
  1207.4 2.2 convolution_bitcast_fusion.4
  1209.7 69.8 %all-reduce.41.cloned.1.call-done = f32[512,256]{0,1:T(8,128)} async-done(((f32[512,256]{0,1:T(8,128)}), f32[512,256]{0,1:T(8,128)}) %all-reduce.41.cloned.1.call-update) | async-done | bytes 524304 | tf_op jit(solution)/shard_map/psum | solution.py:108
  1279.6 2.3 convolution_bitcast_fusion.3
  1281.9 66.4 %all-reduce.43.cloned.1.call-done = f32[512,256]{0,1:T(8,128)} async-done(((f32[512,256]{0,1:T(8,128)}), f32[512,256]{0,1:T(8,128)}) %all-reduce.43.cloned.1.call-update) | async-done | bytes 524304 | tf_op jit(solution)/shard_map/psum | solution.py:108
  1349.1 2.2 convolution_bitcast_fusion.2
  1351.3 70.0 %all-reduce.45.cloned.1.call-done = f32[512,256]{0,1:T(8,128)} async-done(((f32[512,256]{0,1:T(8,128)}), f32[512,256]{0,1:T(8,128)}) %all-reduce.45.cloned.1.call-update) | async-done | bytes 524304 | tf_op jit(solution)/shard_map/psum | solution.py:108
  1421.3 2.2 convolution_bitcast_fusion.1
  1423.6 67.7 %all-reduce.47.cloned.1.call-done = f32[512,256]{0,1:T(8,128)} async-done(((f32[512,256]{0,1:T(8,128)}), f32[512,256]{0,1:T(8,128)}) %all-reduce.47.cloned.1.call-update) | async-done | bytes 524304 | tf_op jit(solution)/shard_map/psum | solution.py:108
  1491.3 5.5 conditional.31
  1491.3 2.1 copy.73
  1493.4 2.4 fusion.16
  1497.6 26.7 %all-gather.2.cloned.1.call-done = bf16[4096,256]{1,0:T(8,128)(2,1)} async-done(((bf16[512,256]{1,0:T(8,128)(2,1)}), bf16[4096,256]{1,0:T(8,128)(2,1)}) %all-gather.2.cloned.1.call-update) | async-done | bytes 2097168 | tf_op jit(solution)/shard_map/all_gather | solution.py:125
  1524.4 3.5 collective-permute-start.2
  1527.8 5.7 collective-permute-start.3
  1533.7 42.1 %collective-permute-done.2 = bf16[4096,256]{1,0:T(8,128)(2,1)} collective-permute-done((bf16[4096,256]{1,0:T(8,128)(2,1)}, bf16[4096,256]{1,0:T(8,128)(2,1)}, u32[]{:S(2)}, u32[]{:S(2)}) %collective-permute-start.2) | collective-permute-done | bytes 2097184 | tf_op jit(solution)/shard_map/ppermute | solution.py:18
  1575.9 90.4 %collective-permute-done.3 = bf16[4096,256]{1,0:T(8,128)(2,1)} collective-permute-done((bf16[4096,256]{1,0:T(8,128)(2,1)}, bf16[4096,256]{1,0:T(8,128)(2,1)}, u32[]{:S(2)}, u32[]{:S(2)}) %collective-permute-start.3) | collective-permute-done | bytes 2097184 | tf_op jit(solution)/shard_map/ppermute | solution.py:18
  1666.2 6.4 pad_maximum_fusion
  1672.7 10.5 reshape.571
  1683.2 4.9 gather_fusion
  1688.4 3.8 fusion.19
  1692.2 2.3 copy.76
  (105 shorter events, 22.4 us)
Async XLA Ops:
  7.2 1.7 copy-start
  7.2 367.2 %reduce-scatter.2.cloned.1.call-start = ((), (), s32[]{:S(2)}) async-start(), calls=%async_computation.1 | async-start | bytes 4718592 | tf_op jit(solution)/shard_map/reduce_scatter | solution.py:68
  8.9 3.0 copy-start.4
  10.9 1.0 copy-start.5
  47.4 96.2 %collective-permute-start = (f32[4096,256]{0,1:T(8,128)}, f32[4096,256]{0,1:T(8,128)}, u32[]{:S(2)}, u32[]{:S(2)}) collective-permute-start(f32[4096,256]{0,1:T(8,128)} %copy.46), channel_id=1, source_target_pairs={{8,0},{16,8},{24,16},{32,24},{40,32},{48,40},{56,48},{64,56},{72,6... | collective-permute-start | bytes 12582920 | tf_op jit(solution)/shard_map/ppermute | solution.py:18
  60.1 175.4 %collective-permute-start.1 = (f32[4096,256]{0,1:T(8,128)}, f32[4096,256]{0,1:T(8,128)}, u32[]{:S(2)}, u32[]{:S(2)}) collective-permute-start(f32[4096,256]{0,1:T(8,128)} %copy.48), channel_id=1, source_target_pairs={{16,0},{24,8},{32,16},{40,24},{48,32},{56,40},{64,48},{72,56},{80,... | collective-permute-start | bytes 12582920 | tf_op jit(solution)/shard_map/ppermute | solution.py:18
  243.3 0.9 copy-start.7
  243.3 133.0 %copy-start.1 = (bf16[512,512]{1,0:T(8,128)(2,1)S(1)}, bf16[512,512]{1,0:T(8,128)(2,1)}, u32[]{:S(2)}) copy-start(bf16[512,512]{1,0:T(8,128)(2,1)} %param.78) | copy-start | bytes 1572868
  243.3 199.4 %all-reduce.17.cloned.1.call-start = ((), (), s32[]{:S(2)}) async-start(), calls=%async_computation.2 | async-start | bytes 524288 | tf_op jit(solution)/shard_map/psum | solution.py:23
  378.8 131.2 %all-reduce.19.cloned.1.call-start = ((), (), s32[]{:S(2)}) async-start(), calls=%async_computation.3 | async-start | bytes 524288 | tf_op jit(solution)/shard_map/psum | solution.py:23
  445.2 132.2 %all-reduce.21.cloned.1.call-start = ((), (), s32[]{:S(2)}) async-start(), calls=%async_computation.4 | async-start | bytes 524288 | tf_op jit(solution)/shard_map/psum | solution.py:23
  513.0 131.4 %all-reduce.23.cloned.1.call-start = ((), (), s32[]{:S(2)}) async-start(), calls=%async_computation.5 | async-start | bytes 524288 | tf_op jit(solution)/shard_map/psum | solution.py:23
  580.0 131.8 %all-reduce.25.cloned.1.call-start = ((), (), s32[]{:S(2)}) async-start(), calls=%async_computation.6 | async-start | bytes 524288 | tf_op jit(solution)/shard_map/psum | solution.py:23
  647.5 131.5 %all-reduce.27.cloned.1.call-start = ((), (), s32[]{:S(2)}) async-start(), calls=%async_computation.7 | async-start | bytes 524288 | tf_op jit(solution)/shard_map/psum | solution.py:23
  714.2 133.4 %all-reduce.29.cloned.1.call-start = ((), (), s32[]{:S(2)}) async-start(), calls=%async_computation.8 | async-start | bytes 524288 | tf_op jit(solution)/shard_map/psum | solution.py:23
  782.0 141.7 %all-reduce.31.cloned.1.call-start = ((), (), s32[]{:S(2)}) async-start(), calls=%async_computation.9 | async-start | bytes 524288 | tf_op jit(solution)/shard_map/psum | solution.py:23
  782.1 141.7 %copy-start.6 = (bf16[512,256]{1,0:T(8,128)(2,1)S(1)}, bf16[512,256]{1,0:T(8,128)(2,1)}, u32[]{:S(2)}) copy-start(bf16[512,256]{1,0:T(8,128)(2,1)} %all-reduce.17.cloned.1.call-done) | copy-start | bytes 786436
  851.4 139.6 %all-reduce.33.cloned.1.call-start = ((), (), s32[]{:S(2)}) async-start(), calls=%async_computation.10 | async-start | bytes 1048576 | tf_op jit(solution)/shard_map/psum | solution.py:108
  853.6 209.4 %all-reduce.35.cloned.1.call-start = ((), (), s32[]{:S(2)}) async-start(), calls=%async_computation.11 | async-start | bytes 1048576 | tf_op jit(solution)/shard_map/psum | solution.py:108
  994.0 141.4 %all-reduce.37.cloned.1.call-start = ((), (), s32[]{:S(2)}) async-start(), calls=%async_computation.12 | async-start | bytes 1048576 | tf_op jit(solution)/shard_map/psum | solution.py:108
  1066.0 140.7 %all-reduce.39.cloned.1.call-start = ((), (), s32[]{:S(2)}) async-start(), calls=%async_computation.13 | async-start | bytes 1048576 | tf_op jit(solution)/shard_map/psum | solution.py:108
  1135.4 72.0 %copy-start.2 = (bf16[512,256]{1,0:T(8,128)(2,1)}, bf16[512,256]{1,0:T(8,128)(2,1)S(1)}, u32[]{:S(2)}) copy-start(bf16[512,256]{1,0:T(8,128)(2,1)S(1)} %get-tuple-element.460) | copy-start | bytes 786436
  1137.7 141.8 %all-reduce.41.cloned.1.call-start = ((), (), s32[]{:S(2)}) async-start(), calls=%async_computation.14 | async-start | bytes 1048576 | tf_op jit(solution)/shard_map/psum | solution.py:108
  1209.7 138.6 %all-reduce.43.cloned.1.call-start = ((), (), s32[]{:S(2)}) async-start(), calls=%async_computation.15 | async-start | bytes 1048576 | tf_op jit(solution)/shard_map/psum | solution.py:108
  1279.6 69.5 %copy-start.3 = (bf16[512,256]{1,0:T(8,128)(2,1)}, bf16[512,256]{1,0:T(8,128)(2,1)S(1)}, u32[]{:S(2)}) copy-start(bf16[512,256]{1,0:T(8,128)(2,1)S(1)} %get-tuple-element.462) | copy-start | bytes 786436
  1281.9 139.4 %all-reduce.45.cloned.1.call-start = ((), (), s32[]{:S(2)}) async-start(), calls=%async_computation.16 | async-start | bytes 1048576 | tf_op jit(solution)/shard_map/psum | solution.py:108
  1351.3 140.1 %all-reduce.47.cloned.1.call-start = ((), (), s32[]{:S(2)}) async-start(), calls=%async_computation.17 | async-start | bytes 1048576 | tf_op jit(solution)/shard_map/psum | solution.py:108
  1423.5 100.8 %all-gather.2.cloned.1.call-start = ((), (), s32[]{:S(2)}) async-start(), calls=%async_computation.18 | async-start | bytes 2359296 | tf_op jit(solution)/shard_map/all_gather | solution.py:125
  1524.4 51.5 %collective-permute-start.2 = (bf16[4096,256]{1,0:T(8,128)(2,1)}, bf16[4096,256]{1,0:T(8,128)(2,1)}, u32[]{:S(2)}, u32[]{:S(2)}) collective-permute-start(bf16[4096,256]{1,0:T(8,128)(2,1)} %all-gather.2.cloned.1.call-done), channel_id=1, source_target_pairs={{0,8},{8,16},{16,24},{24,32},{32,40},{40,48},{48,56},{56,64},{64,7... | collective-permute-start | bytes 6291464 | tf_op jit(solution)/shard_map/ppermute | solution.py:18
  1527.8 138.4 %collective-permute-start.3 = (bf16[4096,256]{1,0:T(8,128)(2,1)}, bf16[4096,256]{1,0:T(8,128)(2,1)}, u32[]{:S(2)}, u32[]{:S(2)}) collective-permute-start(bf16[4096,256]{1,0:T(8,128)(2,1)} %all-gather.2.cloned.1.call-done), channel_id=1, source_target_pairs={{0,16},{8,24},{16,32},{24,40},{32,48},{40,56},{48,64},{56,72},{64,... | collective-permute-start | bytes 6291464 | tf_op jit(solution)/shard_map/ppermute | solution.py:18
Sparse Core Ops, SparseCore 0:
  243.5 130.9 reduce-scatter.1
  378.9 63.8 all-reduce.16
  445.8 64.1 all-reduce.18
  513.1 64.2 all-reduce.20
  580.3 64.1 all-reduce.22
  647.6 64.1 all-reduce.24
  714.8 64.1 all-reduce.26
  782.2 65.4 all-reduce.28
  851.5 72.2 all-reduce.30
  926.0 65.0 all-reduce.32
  994.1 68.8 all-reduce.34
  1066.1 69.2 all-reduce.36
  1137.9 68.7 all-reduce.38
  1209.8 69.7 all-reduce.40
  1282.0 66.2 all-reduce.42
  1351.4 69.8 all-reduce.44
  1423.7 67.6 all-reduce.46
  1497.7 26.5 all-gather.1
where the time goes:
time: 1700 us
  waiting for transfers between devices  1520 us (89%)
  local copies, waits for them, and re-layouts  73.3 us (4%)
  matrix products  52.2 us (3%)
  other arithmetic  24.6 us (1%)
  starting transfers between devices  20 us (1%)
    psum x8, waiting for transfers between devices, shards(): summed_later = lax.psum(partial_term, 'sub')  548 us
    psum x8, waiting for transfers between devices, broadcast(): return lax.psum(jnp.where(mine, shard, jnp.zeros_like(shard)), axis)  522 us
    ppermute x4, waiting for transfers between devices, passed_along(): return lax.ppermute(block, axis, route)  289 us
    reduce_scatter x1, waiting for transfers between devices, shards(): lax.psum_scatter(route_forward(spilled), 'sub', scatter_dimension=0, tile...  130 us
  transfers between devices with their start and end apart: 22, of which 22 were waited for; matrix products, arithmetic and copies ran while one was open for 1% of the time, Pallas kernels for 0%

commit v1 on v0

--- a/solution.py
+++ b/solution.py
@@ -10,6 +10,7 @@
 KB = 4
 SPAN = 3
 exact_precision = lax.Precision.HIGHEST
+close_rings = lambda x0, peer_axis: jnp.sum(lax.all_gather(x0, peer_axis), axis=0)
 
 
 def passed_along(block, axis, distance):
@@ -105,7 +106,7 @@
             (((0,), (0,)), ((), ())),
             preferred_element_type=jnp.float32,
         )
-        summed_later = lax.psum(partial_term, "sub")
+        summed_later = close_rings(partial_term, "sub")
 
         def back_block():
             bracket = forward_store[local_col].astype(jnp.float32) - summed_later

time: 1700 us -> 1520 us (0.89)
  waiting for transfers between devices: 1520 us -> 1320 us
    psum x8 -> x0, waiting for transfers between devices: 548 us -> none  [shards(): summed_later = lax.psum(partial_term, 'sub')]
    all_gather x0 -> x8, waiting for transfers between devices: none -> 356 us  [lax.all_gather(x0, peer_axis)]
  transfers between devices with their start and end apart: 22 -> 22, of which waited for: 22 -> 22; matrix products, arithmetic and copies ran while one was open for 1% -> 2% of each run, Pallas kernels for 0% -> 0%
where the time goes in v1:
time: 1520 us
  waiting for transfers between devices  1320 us (87%)
  local copies, waits for them, and re-layouts  77 us (5%)
  matrix products  52.2 us (3%)
  other arithmetic  27.9 us (2%)
  starting transfers between devices  20.3 us (1%)
    psum x8, waiting for transfers between devices, broadcast(): return lax.psum(jnp.where(mine, shard, jnp.zeros_like(shard)), axis)  522 us
    all_gather x8, waiting for transfers between devices, lax.all_gather(x0, peer_axis)  356 us
    ppermute x4, waiting for transfers between devices, passed_along(): return lax.ppermute(block, axis, route)  289 us
    reduce_scatter x1, waiting for transfers between devices, shards(): lax.psum_scatter(route_forward(spilled), 'sub', scatter_dimension=0, tile...  130 us
  transfers between devices with their start and end apart: 22, of which 22 were waited for; matrix products, arithmetic and copies ran while one was open for 2% of the time, Pallas kernels for 0%

profile of v1, /device:TPU:34, one launch (start us, length us, event | category | flops | bytes accessed | tf_op | source)
XLA Modules:
  0.0 1516.1 jit_solution(1771210512960494270)
XLA Ops:
  8.9 2.0 convolution_convert_fusion.17
  13.4 2.6 copy.45
  16.0 2.4 reshape.570
  18.4 9.1 fusion.50
  27.5 9.4 fusion.57
  36.9 4.9 squeeze.31
  41.8 5.7 copy.46
  47.4 2.0 collective-permute-start
  49.4 5.0 squeeze.32
  54.4 5.6 copy.48
  60.1 8.2 collective-permute-start.1
  68.2 5.0 squeeze.29
  73.2 5.6 copy.47
  78.8 64.7 %collective-permute-done = f32[4096,256]{0,1:T(8,128)} collective-permute-done((f32[4096,256]{0,1:T(8,128)}, f32[4096,256]{0,1:T(8,128)}, u32[]{:S(2)}, u32[]{:S(2)}) %collective-permute-start) | collective-permute-done | bytes 4194336 | tf_op jit(solution)/shard_map/ppermute | solution.py:19
  143.6 91.9 %collective-permute-done.1 = f32[4096,256]{0,1:T(8,128)} collective-permute-done((f32[4096,256]{0,1:T(8,128)}, f32[4096,256]{0,1:T(8,128)}, u32[]{:S(2)}, u32[]{:S(2)}) %collective-permute-start.1) | collective-permute-done | bytes 4194336 | tf_op jit(solution)/shard_map/ppermute | solution.py:19
  235.5 7.8 add_add_fusion
  244.4 130.0 %reduce-scatter.2.cloned.1.call-done = f32[512,256]{0,1:T(8,128)} async-done(((f32[4096,256]{0,1:T(8,128)}), f32[512,256]{0,1:T(8,128)}) %reduce-scatter.2.cloned.1.call-update) | async-done | bytes 524304 | tf_op jit(solution)/shard_map/reduce_scatter | solution.py:69
  374.4 1.9 fusion.45
  376.4 1.7 conditional.16
  376.4 1.7 convolution_convert_fusion
  378.9 63.9 %all-reduce.9.cloned.1.call-done = bf16[512,256]{1,0:T(8,128)(2,1)} async-done(((bf16[512,256]{1,0:T(8,128)(2,1)}), bf16[512,256]{1,0:T(8,128)(2,1)}) %all-reduce.9.cloned.1.call-update) | async-done | bytes 262160 | tf_op jit(solution)/shard_map/psum | solution.py:24
  442.8 1.6 fusion.20
  445.3 64.7 %all-reduce.11.cloned.1.call-done = bf16[512,256]{1,0:T(8,128)(2,1)} async-done(((bf16[512,256]{1,0:T(8,128)(2,1)}), bf16[512,256]{1,0:T(8,128)(2,1)}) %all-reduce.11.cloned.1.call-update) | async-done | bytes 262160 | tf_op jit(solution)/shard_map/psum | solution.py:24
  510.0 2.3 fusion.21
  513.1 64.3 %all-reduce.13.cloned.1.call-done = bf16[512,256]{1,0:T(8,128)(2,1)} async-done(((bf16[512,256]{1,0:T(8,128)(2,1)}), bf16[512,256]{1,0:T(8,128)(2,1)}) %all-reduce.13.cloned.1.call-update) | async-done | bytes 262160 | tf_op jit(solution)/shard_map/psum | solution.py:24
  580.1 64.4 %all-reduce.15.cloned.1.call-done = bf16[512,256]{1,0:T(8,128)(2,1)} async-done(((bf16[512,256]{1,0:T(8,128)(2,1)}), bf16[512,256]{1,0:T(8,128)(2,1)}) %all-reduce.15.cloned.1.call-update) | async-done | bytes 262160 | tf_op jit(solution)/shard_map/psum | solution.py:24
  644.5 2.3 fusion.23
  647.6 64.2 %all-reduce.17.cloned.1.call-done = bf16[512,256]{1,0:T(8,128)(2,1)} async-done(((bf16[512,256]{1,0:T(8,128)(2,1)}), bf16[512,256]{1,0:T(8,128)(2,1)}) %all-reduce.17.cloned.1.call-update) | async-done | bytes 262160 | tf_op jit(solution)/shard_map/psum | solution.py:24
  711.8 1.6 fusion.24
  714.3 64.7 %all-reduce.19.cloned.1.call-done = bf16[512,256]{1,0:T(8,128)(2,1)} async-done(((bf16[512,256]{1,0:T(8,128)(2,1)}), bf16[512,256]{1,0:T(8,128)(2,1)}) %all-reduce.19.cloned.1.call-update) | async-done | bytes 262160 | tf_op jit(solution)/shard_map/psum | solution.py:24
  779.0 2.3 fusion.25
  782.1 65.5 %all-reduce.21.cloned.1.call-done = bf16[512,256]{1,0:T(8,128)(2,1)} async-done(((bf16[512,256]{1,0:T(8,128)(2,1)}), bf16[512,256]{1,0:T(8,128)(2,1)}) %all-reduce.21.cloned.1.call-update) | async-done | bytes 262160 | tf_op jit(solution)/shard_map/psum | solution.py:24
  847.6 2.3 convolution_bitcast_fusion.9
  851.4 2.2 convolution_bitcast_fusion.8
  853.7 70.1 %all-reduce.23.cloned.1.call-done = bf16[512,256]{1,0:T(8,128)(2,1)} async-done(((bf16[512,256]{1,0:T(8,128)(2,1)}), bf16[512,256]{1,0:T(8,128)(2,1)}) %all-reduce.23.cloned.1.call-update) | async-done | bytes 262160 | tf_op jit(solution)/shard_map/psum | solution.py:24
  923.9 35.4 %all-gather.20.cloned.1.call-done = f32[4096,256]{0,1:T(8,128)} async-done(((f32[512,256]{0,1:T(8,128)}), f32[4096,256]{0,1:T(8,128)}) %all-gather.20.cloned.1.call-update) | async-done | bytes 4194320 | tf_op jit(solution)/shard_map/all_gather | solution.py:13
  960.1 2.2 convolution_bitcast_fusion.7
  962.3 44.5 %all-gather.22.cloned.1.call-done = f32[4096,256]{0,1:T(8,128)} async-done(((f32[512,256]{0,1:T(8,128)}), f32[4096,256]{0,1:T(8,128)}) %all-gather.22.cloned.1.call-update) | async-done | bytes 4194320 | tf_op jit(solution)/shard_map/all_gather | solution.py:13
  1007.6 2.2 convolution_bitcast_fusion.6
  1009.8 45.5 %all-gather.24.cloned.1.call-done = f32[4096,256]{0,1:T(8,128)} async-done(((f32[512,256]{0,1:T(8,128)}), f32[4096,256]{0,1:T(8,128)}) %all-gather.24.cloned.1.call-update) | async-done | bytes 4194320 | tf_op jit(solution)/shard_map/all_gather | solution.py:13
  1055.3 2.3 convolution_bitcast_fusion.5
  1057.7 47.1 %all-gather.26.cloned.1.call-done = f32[4096,256]{0,1:T(8,128)} async-done(((f32[512,256]{0,1:T(8,128)}), f32[4096,256]{0,1:T(8,128)}) %all-gather.26.cloned.1.call-update) | async-done | bytes 4194320 | tf_op jit(solution)/shard_map/all_gather | solution.py:13
  1105.6 2.2 convolution_bitcast_fusion.4
  1107.8 46.5 %all-gather.28.cloned.1.call-done = f32[4096,256]{0,1:T(8,128)} async-done(((f32[512,256]{0,1:T(8,128)}), f32[4096,256]{0,1:T(8,128)}) %all-gather.28.cloned.1.call-update) | async-done | bytes 4194320 | tf_op jit(solution)/shard_map/all_gather | solution.py:13
  1154.4 2.3 convolution_bitcast_fusion.3
  1156.7 45.9 %all-gather.30.cloned.1.call-done = f32[4096,256]{0,1:T(8,128)} async-done(((f32[512,256]{0,1:T(8,128)}), f32[4096,256]{0,1:T(8,128)}) %all-gather.30.cloned.1.call-update) | async-done | bytes 4194320 | tf_op jit(solution)/shard_map/all_gather | solution.py:13
  1203.3 2.2 convolution_bitcast_fusion.2
  1205.6 45.3 %all-gather.32.cloned.1.call-done = f32[4096,256]{0,1:T(8,128)} async-done(((f32[512,256]{0,1:T(8,128)}), f32[4096,256]{0,1:T(8,128)}) %all-gather.32.cloned.1.call-update) | async-done | bytes 4194320 | tf_op jit(solution)/shard_map/all_gather | solution.py:13
  1250.9 2.2 convolution_bitcast_fusion.1
  1253.2 46.0 %all-gather.34.cloned.1.call-done = f32[4096,256]{0,1:T(8,128)} async-done(((f32[512,256]{0,1:T(8,128)}), f32[4096,256]{0,1:T(8,128)}) %all-gather.34.cloned.1.call-update) | async-done | bytes 4194320 | tf_op jit(solution)/shard_map/all_gather | solution.py:13
  1299.2 12.5 conditional.31
  1299.2 5.7 copy.111
  1304.8 3.3 reduce_sum.79
  1308.2 2.4 fusion.16
  1312.4 26.7 %all-gather.18.cloned.1.call-done = bf16[4096,256]{1,0:T(8,128)(2,1)} async-done(((bf16[512,256]{1,0:T(8,128)(2,1)}), bf16[4096,256]{1,0:T(8,128)(2,1)}) %all-gather.18.cloned.1.call-update) | async-done | bytes 2097168 | tf_op jit(solution)/shard_map/all_gather | solution.py:126
  1339.1 3.5 collective-permute-start.2
  1342.6 5.9 collective-permute-start.3
  1348.8 41.9 %collective-permute-done.2 = bf16[4096,256]{1,0:T(8,128)(2,1)} collective-permute-done((bf16[4096,256]{1,0:T(8,128)(2,1)}, bf16[4096,256]{1,0:T(8,128)(2,1)}, u32[]{:S(2)}, u32[]{:S(2)}) %collective-permute-start.2) | collective-permute-done | bytes 2097184 | tf_op jit(solution)/shard_map/ppermute | solution.py:19
  1390.6 90.4 %collective-permute-done.3 = bf16[4096,256]{1,0:T(8,128)(2,1)} collective-permute-done((bf16[4096,256]{1,0:T(8,128)(2,1)}, bf16[4096,256]{1,0:T(8,128)(2,1)}, u32[]{:S(2)}, u32[]{:S(2)}) %collective-permute-start.3) | collective-permute-done | bytes 2097184 | tf_op jit(solution)/shard_map/ppermute | solution.py:19
  1481.0 6.4 pad_maximum_fusion
  1487.5 10.5 reshape.571
  1498.0 4.9 gather_fusion
  1503.1 3.8 fusion.19
  1507.0 2.3 copy.76
  (106 shorter events, 24.1 us)
Async XLA Ops:
  7.2 1.7 copy-start
  7.2 367.2 %reduce-scatter.2.cloned.1.call-start = ((), (), s32[]{:S(2)}) async-start(), calls=%async_computation.1 | async-start | bytes 4718592 | tf_op jit(solution)/shard_map/reduce_scatter | solution.py:69
  8.9 3.0 copy-start.4
  10.9 1.0 copy-start.5
  47.4 96.2 %collective-permute-start = (f32[4096,256]{0,1:T(8,128)}, f32[4096,256]{0,1:T(8,128)}, u32[]{:S(2)}, u32[]{:S(2)}) collective-permute-start(f32[4096,256]{0,1:T(8,128)} %copy.46), channel_id=1, source_target_pairs={{8,0},{16,8},{24,16},{32,24},{40,32},{48,40},{56,48},{64,56},{72,6... | collective-permute-start | bytes 12582920 | tf_op jit(solution)/shard_map/ppermute | solution.py:19
  60.1 175.4 %collective-permute-start.1 = (f32[4096,256]{0,1:T(8,128)}, f32[4096,256]{0,1:T(8,128)}, u32[]{:S(2)}, u32[]{:S(2)}) collective-permute-start(f32[4096,256]{0,1:T(8,128)} %copy.48), channel_id=1, source_target_pairs={{16,0},{24,8},{32,16},{40,24},{48,32},{56,40},{64,48},{72,56},{80,... | collective-permute-start | bytes 12582920 | tf_op jit(solution)/shard_map/ppermute | solution.py:19
  243.3 0.9 copy-start.7
  243.3 133.0 %copy-start.1 = (bf16[512,512]{1,0:T(8,128)(2,1)S(1)}, bf16[512,512]{1,0:T(8,128)(2,1)}, u32[]{:S(2)}) copy-start(bf16[512,512]{1,0:T(8,128)(2,1)} %param.78) | copy-start | bytes 1572868
  243.3 199.4 %all-reduce.9.cloned.1.call-start = ((), (), s32[]{:S(2)}) async-start(), calls=%async_computation.2 | async-start | bytes 524288 | tf_op jit(solution)/shard_map/psum | solution.py:24
  378.8 131.2 %all-reduce.11.cloned.1.call-start = ((), (), s32[]{:S(2)}) async-start(), calls=%async_computation.3 | async-start | bytes 524288 | tf_op jit(solution)/shard_map/psum | solution.py:24
  445.2 132.2 %all-reduce.13.cloned.1.call-start = ((), (), s32[]{:S(2)}) async-start(), calls=%async_computation.4 | async-start | bytes 524288 | tf_op jit(solution)/shard_map/psum | solution.py:24
  513.0 131.4 %all-reduce.15.cloned.1.call-start = ((), (), s32[]{:S(2)}) async-start(), calls=%async_computation.5 | async-start | bytes 524288 | tf_op jit(solution)/shard_map/psum | solution.py:24
  580.0 131.8 %all-reduce.17.cloned.1.call-start = ((), (), s32[]{:S(2)}) async-start(), calls=%async_computation.6 | async-start | bytes 524288 | tf_op jit(solution)/shard_map/psum | solution.py:24
  647.5 131.5 %all-reduce.19.cloned.1.call-start = ((), (), s32[]{:S(2)}) async-start(), calls=%async_computation.7 | async-start | bytes 524288 | tf_op jit(solution)/shard_map/psum | solution.py:24
  714.2 133.4 %all-reduce.21.cloned.1.call-start = ((), (), s32[]{:S(2)}) async-start(), calls=%async_computation.8 | async-start | bytes 524288 | tf_op jit(solution)/shard_map/psum | solution.py:24
  782.0 141.8 %all-reduce.23.cloned.1.call-start = ((), (), s32[]{:S(2)}) async-start(), calls=%async_computation.9 | async-start | bytes 524288 | tf_op jit(solution)/shard_map/psum | solution.py:24
  782.1 141.7 %copy-start.6 = (bf16[512,256]{1,0:T(8,128)(2,1)S(1)}, bf16[512,256]{1,0:T(8,128)(2,1)}, u32[]{:S(2)}) copy-start(bf16[512,256]{1,0:T(8,128)(2,1)} %all-reduce.9.cloned.1.call-done) | copy-start | bytes 786436
  851.4 107.9 %all-gather.20.cloned.1.call-start = ((), (), s32[]{:S(2)}) async-start(), calls=%async_computation.11 | async-start | bytes 4718592 | tf_op jit(solution)/shard_map/all_gather | solution.py:13
  853.6 153.2 %all-gather.22.cloned.1.call-start = ((), (), s32[]{:S(2)}) async-start(), calls=%async_computation.12 | async-start | bytes 4718592 | tf_op jit(solution)/shard_map/all_gather | solution.py:13
  962.3 93.0 %all-gather.24.cloned.1.call-start = ((), (), s32[]{:S(2)}) async-start(), calls=%async_computation.13 | async-start | bytes 4718592 | tf_op jit(solution)/shard_map/all_gather | solution.py:13
  1009.8 95.0 %all-gather.26.cloned.1.call-start = ((), (), s32[]{:S(2)}) async-start(), calls=%async_computation.14 | async-start | bytes 4718592 | tf_op jit(solution)/shard_map/all_gather | solution.py:13
  1055.3 49.5 %copy-start.2 = (bf16[512,256]{1,0:T(8,128)(2,1)}, bf16[512,256]{1,0:T(8,128)(2,1)S(1)}, u32[]{:S(2)}) copy-start(bf16[512,256]{1,0:T(8,128)(2,1)S(1)} %get-tuple-element.478) | copy-start | bytes 786436
  1057.7 96.7 %all-gather.28.cloned.1.call-start = ((), (), s32[]{:S(2)}) async-start(), calls=%async_computation.15 | async-start | bytes 4718592 | tf_op jit(solution)/shard_map/all_gather | solution.py:13
  1107.8 94.8 %all-gather.30.cloned.1.call-start = ((), (), s32[]{:S(2)}) async-start(), calls=%async_computation.16 | async-start | bytes 4718592 | tf_op jit(solution)/shard_map/all_gather | solution.py:13
  1154.4 48.2 %copy-start.3 = (bf16[512,256]{1,0:T(8,128)(2,1)}, bf16[512,256]{1,0:T(8,128)(2,1)S(1)}, u32[]{:S(2)}) copy-start(bf16[512,256]{1,0:T(8,128)(2,1)S(1)} %get-tuple-element.482) | copy-start | bytes 786436
  1156.7 94.2 %all-gather.32.cloned.1.call-start = ((), (), s32[]{:S(2)}) async-start(), calls=%async_computation.17 | async-start | bytes 4718592 | tf_op jit(solution)/shard_map/all_gather | solution.py:13
  1205.5 93.6 %all-gather.34.cloned.1.call-start = ((), (), s32[]{:S(2)}) async-start(), calls=%async_computation.18 | async-start | bytes 4718592 | tf_op jit(solution)/shard_map/all_gather | solution.py:13
  1253.1 86.0 %all-gather.18.cloned.1.call-start = ((), (), s32[]{:S(2)}) async-start(), calls=%async_computation.10 | async-start | bytes 2359296 | tf_op jit(solution)/shard_map/all_gather | solution.py:126
  1339.1 51.5 %collective-permute-start.2 = (bf16[4096,256]{1,0:T(8,128)(2,1)}, bf16[4096,256]{1,0:T(8,128)(2,1)}, u32[]{:S(2)}, u32[]{:S(2)}) collective-permute-start(bf16[4096,256]{1,0:T(8,128)(2,1)} %all-gather.18.cloned.1.call-done), channel_id=1, source_target_pairs={{0,8},{8,16},{16,24},{24,32},{32,40},{40,48},{48,56},{56,64},{64,7... | collective-permute-start | bytes 6291464 | tf_op jit(solution)/shard_map/ppermute | solution.py:19
  1342.6 138.4 %collective-permute-start.3 = (bf16[4096,256]{1,0:T(8,128)(2,1)}, bf16[4096,256]{1,0:T(8,128)(2,1)}, u32[]{:S(2)}, u32[]{:S(2)}) collective-permute-start(bf16[4096,256]{1,0:T(8,128)(2,1)} %all-gather.18.cloned.1.call-done), channel_id=1, source_target_pairs={{0,16},{8,24},{16,32},{24,40},{32,48},{40,56},{48,64},{56,72},{64,... | collective-permute-start | bytes 6291464 | tf_op jit(solution)/shard_map/ppermute | solution.py:19
Sparse Core Ops, SparseCore 0:
  243.5 130.9 reduce-scatter.1
  378.9 63.8 all-reduce.8
  445.8 64.1 all-reduce.10
  513.1 64.2 all-reduce.12
  580.3 64.1 all-reduce.14
  647.6 64.1 all-reduce.16
  714.8 64.1 all-reduce.18
  782.2 65.4 all-reduce.20
  851.5 72.2 all-reduce.22
  925.5 33.8 all-gather.19
  962.4 44.3 all-gather.21
  1009.9 45.3 all-gather.23
  1057.8 46.9 all-gather.25
  1107.9 46.3 all-gather.27
  1156.8 45.7 all-gather.29
  1205.7 45.1 all-gather.31
  1253.2 45.8 all-gather.33
  1312.5 26.5 all-gather.17
